TPU v7x, 32 devices: a whole 2x2x4 slice. The times are simulated.
32 devices in a mesh: req: 8 (over y, x, core), tp: 4 (over z).
Axes of the slice: x: 2, y: 2, z: 4, core: 2. Of those that a mesh axis runs over, the one named last changes fastest.
Arguments:
- new_query: bfloat16 [1024, 2560], P('req', 'tp'), may hold values from -64 to 64
- new_keyval: bfloat16 [1024, 1280], P('req', 'tp'), may hold values from -24 to 24
- residual_in: bfloat16 [1024, 2560], P('req'), may hold values from -64 to 64
- leaf_cache: bfloat16 [128, 32, 1280], P('req', None, 'tp'), may hold values from -6 to 6
- leaf_length: int32 [128], P('req'), may hold values from 1 to 32
- new_counts: int32 [8, 16], P('req'), may hold values from 1 to 16, as said below
- request_mid: int32 [128], P('req'), may hold values from 0 to 5
- mid_root: int32 [6], replicated, may hold values from 0 to 1, as said below
- node_length: int32 [8], replicated, may hold values from 1 to 1744, as said below
- prefix_pool: bfloat16 [256, 16, 1280], P('req', None, 'tp'), may hold values from -6 to 6
- page_node: int32 [256], P('req'), may hold values from -1 to 7, as said below
- page_rank: int32 [256], P('req'), may hold values from 0 to 108, as said below
- out_weight: bfloat16 [2560, 2560], P('tp'), may hold values from -0.125 to 0.125
- norm_gain: bfloat16 [2560], replicated, may hold values from 0.5 to 1.5
- gate_weight: bfloat16 [2560, 3584], P(None, 'tp'), may hold values from -0.125 to 0.125
- up_weight: bfloat16 [2560, 3584], P(None, 'tp'), may hold values from -0.125 to 0.125
- down_weight: bfloat16 [3584, 2560], P('tp'), may hold values from -0.09375 to 0.09375
- next_gain: bfloat16 [2560], replicated, may hold values from 0.5 to 1.5
- query_weight: bfloat16 [2560, 2560], P(None, 'tp'), may hold values from -0.125 to 0.125
- keyval_weight: bfloat16 [2560, 1280], P(None, 'tp'), may hold values from -0.125 to 0.125
Outputs:
- attention: bfloat16 [1024, 2560], P('req', 'tp')
- residual_out: bfloat16 [1024, 2560], P(('req', 'tp'))
- next_query: bfloat16 [1024, 2560], P('req', 'tp')
- next_keyval: bfloat16 [1024, 1280], P('req', 'tp')
Inputs may be any that keep to these rules, and one draw needn't show every extreme that they name: `new_counts`: each row sums to 128 and holds one request of exactly 16 new tokens. `mid_root`: each root is the parent of 3 mid-level nodes. `node_length`: A node of k pages has more than 16 * (k - 1) and at most 16 * k prefix tokens; a node with the most pages has exactly 16 * k. `page_node`: every node owns one page or more; 32 pages are free (-1). `page_rank`: the k pages of a node carry the ranks 0 to k - 1, each once; free pages carry 0.
All inputs are finite; a program needn't handle non-finite values.
Results may differ from a plain program's by a relative error of at most 0.015.
Values may be sent and summed in bfloat16 or wider, within the bound.
No kernel may reach another device: no remote copies, remote signals or barrier semaphores. Data moves between devices by JAX's collectives and lax.ppermute only.
A program may use at most 128 MiB of HBM per device.

v0:
```python
import math
import jax
import jax.numpy as jnp
from jax import lax
from jax.sharding import PartitionSpec as P

HD = 80
MAXNEW = 16
ROOTS = 2
MIDS = 6
NODES = 8
MASKED = -1e30
EPSILON = 1e-05


def rms_scale(values_in, gain):
    values = values_in.astype(jnp.float32)
    scale = lax.rsqrt(jnp.mean(values * values, axis=-1, keepdims=True) + EPSILON)
    return (values * scale * gain.astype(jnp.float32)).astype(jnp.bfloat16)


def combine(first, second):
    top_first, total_first, sum_first = first
    top_second, total_second, sum_second = second
    top = jnp.maximum(top_first, top_second)
    factor_first = jnp.exp(top_first - top)
    factor_second = jnp.exp(top_second - top)
    total = total_first * factor_first + total_second * factor_second
    weighted = sum_first * factor_first[..., None] + sum_second * factor_second[..., None]
    return (top, total, weighted)


def attend(queries, keys, values, visible):
    scores = jnp.einsum("nkgd,mkd->nkgm", queries, keys, preferred_element_type=jnp.float32) * (
        1.0 / math.sqrt(HD)
    )
    shown = visible[:, None, None, :]
    scores = jnp.where(shown, scores, MASKED)
    top = jnp.max(scores, axis=-1)
    raised = jnp.where(shown, jnp.exp(scores - top[..., None]), 0.0)
    total = jnp.sum(raised, axis=-1)
    weighted = jnp.einsum(
        "nkgm,mkd->nkgd", raised.astype(jnp.bfloat16), values, preferred_element_type=jnp.float32
    )
    return (top, total, weighted)


def pool_split(pages_in, node_of_page, rank_of_page):
    page_count = pages_in.shape[0]
    page_size = pages_in.shape[1]
    flat = pages_in.reshape(page_count * page_size, pages_in.shape[2] // (2 * HD), 2, HD)
    key_node = jnp.repeat(node_of_page, page_size, total_repeat_length=page_count * page_size)
    key_place = (
        rank_of_page[:, None] * page_size + jnp.arange(page_size, dtype=jnp.int32)[None, :]
    ).reshape(page_count * page_size)
    return (flat[:, :, 0], flat[:, :, 1], key_node, key_place)


def shared_visible(token_info, key_node, key_place):
    root_hit = (key_node[None, :] == token_info[:, 0:1]) & (key_place[None, :] < token_info[:, 2:3])
    mid_hit = (key_node[None, :] == token_info[:, 1:2]) & (key_place[None, :] < token_info[:, 3:4])
    return root_hit | mid_hit


def token_tables(counts, request_mid, mid_root, node_length, row_count):
    requests = counts.shape[0]
    starts = jnp.cumsum(counts) - counts
    index = jnp.arange(row_count, dtype=jnp.int32)
    owner = jnp.sum((index[:, None] >= starts[None, :]).astype(jnp.int32), axis=1) - 1
    pick = (owner[:, None] == jnp.arange(requests, dtype=jnp.int32)[None, :]).astype(jnp.int32)
    offset = index - jnp.sum(pick * starts[None, :], axis=1)
    token_mid = jnp.sum(pick * request_mid[None, :], axis=1)
    mid_pick = (token_mid[:, None] == jnp.arange(MIDS, dtype=jnp.int32)[None, :]).astype(jnp.int32)
    token_root = jnp.sum(mid_pick * mid_root[None, :], axis=1)
    mid_node = token_mid + ROOTS
    node_ids = jnp.arange(NODES, dtype=jnp.int32)
    root_len = jnp.sum(
        (token_root[:, None] == node_ids[None, :]).astype(jnp.int32) * node_length[None, :], axis=1
    )
    mid_len = jnp.sum(
        (mid_node[:, None] == node_ids[None, :]).astype(jnp.int32) * node_length[None, :], axis=1
    )
    token_info = jnp.stack([token_root, mid_node, root_len, mid_len], axis=1)
    return (starts, owner, offset, token_info)


def local_part(
    new_query, new_keyval, leaf_cache, leaf_length, counts, starts, owner, offset, kv_local, group
):
    requests = counts.shape[0]
    leaf_slots = leaf_cache.shape[1]
    slot = jnp.arange(MAXNEW, dtype=jnp.int32)
    row_index = jnp.clip(starts[:, None] + slot[None, :], 0, new_query.shape[0] - 1)
    pad_query = new_query[row_index].reshape(requests, MAXNEW, kv_local, group, HD)
    pad_keyval = new_keyval[row_index]
    joined = jnp.concatenate([leaf_cache, pad_keyval], axis=1).reshape(
        requests, leaf_slots + MAXNEW, kv_local, 2, HD
    )
    leaf_ok = jnp.broadcast_to(
        jnp.arange(leaf_slots, dtype=jnp.int32)[None, None, :] < leaf_length[:, None, None],
        (requests, MAXNEW, leaf_slots),
    )
    causal = jnp.broadcast_to(
        slot[None, None, :] <= slot[None, :, None], (requests, MAXNEW, MAXNEW)
    )
    visible = jnp.concatenate([leaf_ok, causal], axis=2)
    part = jax.vmap(attend)(pad_query, joined[:, :, :, 0], joined[:, :, :, 1], visible)
    flat = owner * MAXNEW + offset
    return tuple((item.reshape((requests * MAXNEW,) + item.shape[2:])[flat] for item in part))


def visit_owners(new_query, token_info, prefix_pool, page_node, page_rank, kv_local, group):
    all_query, all_info = (
        lax.all_gather(new_query, "req", axis=0, tiled=True),
        lax.all_gather(token_info, "req", axis=0, tiled=True),
    )
    total_rows = all_query.shape[0]
    block = math.gcd(total_rows, 512)
    keys, values, key_node, key_place = pool_split(prefix_pool, page_node, page_rank)

    def owner_block(items):
        query_block, info_block = items
        heads = query_block.reshape(block, kv_local, group, HD)
        return attend(heads, keys, values, shared_visible(info_block, key_node, key_place))

    part = lax.map(
        owner_block,
        (
            all_query.reshape(total_rows // block, block, all_query.shape[1]),
            all_info.reshape(total_rows // block, block, 4),
        ),
    )
    holders = lax.axis_size("req")
    row_count = total_rows // holders
    part_top, part_total, part_sum = tuple(
        (item.reshape((holders, row_count) + item.shape[2:]) for item in part)
    )
    tops, totals, sums = (
        lax.all_to_all(part_top, "req", split_axis=0, concat_axis=0, tiled=True),
        lax.all_to_all(part_total, "req", split_axis=0, concat_axis=0, tiled=True),
        lax.all_to_all(part_sum, "req", split_axis=0, concat_axis=0, tiled=True),
    )
    top = jnp.max(tops, axis=0)
    factor = jnp.exp(tops - top[None])
    return (top, jnp.sum(totals * factor, axis=0), jnp.sum(sums * factor[..., None], axis=0))


def per_device(
    new_query,
    new_keyval,
    residual_in,
    leaf_cache,
    leaf_length,
    new_counts,
    request_mid,
    mid_root,
    node_length,
    prefix_pool,
    page_node,
    page_rank,
    out_weight,
    norm_gain,
    gate_weight,
    up_weight,
    down_weight,
    next_gain,
    query_weight,
    keyval_weight,
):
    row_count = new_query.shape[0]
    query_width = new_query.shape[1]
    keyval_width = new_keyval.shape[1]
    kv_local = keyval_width // (2 * HD)
    group = query_width // (kv_local * HD)
    counts = new_counts[0]
    starts, owner, offset, token_info = token_tables(
        counts, request_mid, mid_root, node_length, row_count
    )
    shared = visit_owners(new_query, token_info, prefix_pool, page_node, page_rank, kv_local, group)
    local = local_part(
        new_query,
        new_keyval,
        leaf_cache,
        leaf_length,
        counts,
        starts,
        owner,
        offset,
        kv_local,
        group,
    )
    top, total, weighted = combine(shared, local)
    attention = (weighted / total[..., None]).reshape(row_count, query_width).astype(jnp.bfloat16)
    share = row_count // lax.axis_size("tp")
    mine = lax.axis_index("tp") * share
    attn_proj = lax.psum(jnp.dot(attention, out_weight, preferred_element_type=jnp.float32), "tp")
    mixed = (residual_in.astype(jnp.float32) + attn_proj).astype(jnp.bfloat16)
    normed = rms_scale(mixed, norm_gain)
    gate = jnp.dot(normed, gate_weight, preferred_element_type=jnp.float32)
    upward = jnp.dot(normed, up_weight, preferred_element_type=jnp.float32)
    hidden = (jax.nn.silu(gate) * upward).astype(jnp.bfloat16)
    mlp_proj = lax.psum(jnp.dot(hidden, down_weight, preferred_element_type=jnp.float32), "tp")
    layer_rows = (mixed.astype(jnp.float32) + mlp_proj).astype(jnp.bfloat16)
    residual_out = lax.dynamic_slice_in_dim(layer_rows, mine, share, 0)
    final = rms_scale(layer_rows, next_gain)
    next_query = jnp.dot(final, query_weight, preferred_element_type=jnp.float32).astype(
        jnp.bfloat16
    )
    next_keyval = jnp.dot(final, keyval_weight, preferred_element_type=jnp.float32).astype(
        jnp.bfloat16
    )
    return (attention, residual_out, next_query, next_keyval)


def solution(mesh):
    in_specs = (
        P("req", "tp"),
        P("req", "tp"),
        P("req", None),
        P("req", None, "tp"),
        P("req"),
        P("req", None),
        P("req"),
        P(),
        P(),
        P("req", None, "tp"),
        P("req"),
        P("req"),
        P("tp", None),
        P(),
        P(None, "tp"),
        P(None, "tp"),
        P("tp", None),
        P(),
        P(None, "tp"),
        P(None, "tp"),
    )
    out_specs = (P("req", "tp"), P(("req", "tp"), None), P("req", "tp"), P("req", "tp"))
    return jax.shard_map(
        per_device, mesh=mesh, in_specs=in_specs, out_specs=out_specs, check_vma=False
    )
```

profile of v0, /device:TPU:0, one launch (start us, length us, event | category | flops | bytes accessed | tf_op | source)
XLA Modules:
  0.0 375.2 jit_solution(16658785647169500201)
XLA Ops:
  8.0 0.9 copy.127
  10.4 2.1 reshape.441
  12.5 3.1 fusion.62
  16.4 1.8 copy.129
  18.2 1.8 copy.128
  20.8 11.4 %all_gather.6 = s32[1024,4]{0,1:T(4,128)} all-gather(s32[128,4]{0,1:T(4,128)S(1)} %pad_add_fusion.1), channel_id=1, replica_groups=mesh['req'=8,'tp'=4] {'req'}, dimensions={0}, use_global_device_ids=true | all-gather | bytes 18432 | tf_op jit(solution)/shard_map/all_gather | solution.py:115
  33.8 4.2 %compare_select_fusion.2 = (s32[512,1]{0,1:T(1,128)S(1)}, s32[512,1]{0,1:T(1,128)S(1)}) fusion(s32[]{:T(128)} %bitcast.29, s32[]{:T(128)} %bitcast.30, s32[]{:T(128)} %bitcast.31, s32[]{:T(128)} %bitcast.32, s32[]{:T(128)} %bitcast.33, s32[]{:T(128)} %bitcast.35, s32[]{:T(128)} %bitcast.34, s32[512,1]{0,1:T(1,128)S(1)} %bitcast.213, s32[512,1]{0,1:T(1,128)S(1)} %bitcast.212), kind=kLoop, calls=%fused_computation.105 | loop fusion | flops 7168 | bytes 8220 | tf_op jit(solution)/shard_map/jit(_take)/gather | solution.py:52
  38.6 16.0 %select_select_fusion = s32[512]{0:T(512)} fusion(pred[512]{0:T(512)(128)(4,1)S(1)} %get-tuple-element.200, pred[512]{0:T(512)(128)(4,1)S(1)} %get-tuple-element.199, pred[512]{0:T(512)(128)(4,1)S(1)} %get-tuple-element.198, pred[512]{0:T(512)(128)(4,1)S(1)} %get-tuple-element.197, pred[512]{0:T(512)(128)(4,1)S(1)} %get-tuple-element.196, ...), kind=kLoop, calls=%fused_computation.129 | loop fusion | flops 17408 | bytes 19060 | tf_op jit(solution)/shard_map/jit(_take)/select_n | solution.py:52
  54.6 100.4 %while.16 = (s32[]{:T(128)}, f32[2,512,2,4]{1,0,3,2:T(2,128)}, f32[2,512,2,4]{1,0,3,2:T(2,128)}, f32[2,512,2,4,80]{1,0,4,3,2:T(2,128)}, s32[512]{0:T(512)}, /*in...) while((s32[]{:T(128)}, f32[2,512,2,4]{1,0,3,2:T(2,128)}, ...), condition=%wide.region_9.10_spmd.clone, body=%wide.region_6.0_spmd.clone.sunk | while | flops 700178944 | bytes 71092600 | solution.py:126
  56.7 1.2 and_or_fusion.2
  57.8 2.0 constant_dynamic-slice_fusion.3
  59.8 2.2 copy.193
  62.0 5.8 %bitcast_reduce_fusion.2 = (f32[512,2,4]{0,2,1:T(4,128)S(1)}, f32[2,512,4,512]{1,3,2,0:T(8,128)}) fusion(pred[512,512]{0,1:T(8,128)(4,1)S(1)} %and_or_fusion.2, bf16[512,2,4,80]{0,3,2,1:T(8,128)(2,1)} %bitcast.188, bf16[512,2,80]{0,2,1:T(8,128)(2,1)} %get-tuple-element.391), kind=kOutput, calls=%fused_computation.7.clone.1 | convolution fusion | flops 341831680 | bytes 9486336 | tf_op jit(solution)/shard_map/while/body/eval_jaxpr/nkgd,mkd->nkgm/dot_general | solution.py:34
  68.5 1.4 dynamic_update_slice.17
  69.9 4.6 %fusion.85 = f32[512,2,4]{0,2,1:T(4,128)S(1)} fusion(f32[2,512,4,512]{1,3,2,0:T(8,128)} %get-tuple-element.359, f32[512,2,4]{0,2,1:T(4,128)S(1)} %get-tuple-element.358, pred[512,512]{0,1:T(8,128)(4,1)S(1)} %and_or_fusion.2), kind=kLoop, calls=%fused_computation.12.clone.1 | loop fusion | flops 10481664 | bytes 8683520 | tf_op jit(solution)/shard_map/while/body/eval_jaxpr/reduce_sum | solution.py:41
  74.5 1.2 copy-done.1
  75.8 2.3 fusion.86
  78.1 2.4 copy.196
  80.6 24.2 %dynamic_update_slice.19 = f32[2,512,2,4,80]{1,0,4,3,2:T(2,128)} dynamic-update-slice(f32[2,512,2,4,80]{1,0,4,3,2:T(2,128)} %get-tuple-element.375, f32[1,512,2,4,80]{1,0,4,3,2:T(1,128)} %copy.196, s32[]{:T(128)S(6)} %copy.204, s32[]{:T(128)} %constant.138.clone.1..sunk, s32[]{:T(128)} %constant.138.clone.1..sunk, s32[]{:T(128)} %constant.138.clone.1..sunk, s32[]{:T(128)} %constant.138.clone.1..sunk) | dynamic-update-slice | bytes 2621444 | tf_op jit(solution)/shard_map/while/body/jit(dynamic_update_index_in_dim)/dynamic_update_slice | solution.py:126
  106.9 1.2 and_or_fusion.2
  108.1 2.0 constant_dynamic-slice_fusion.3
  110.0 2.2 copy.193
  112.2 5.8 %bitcast_reduce_fusion.2 = (f32[512,2,4]{0,2,1:T(4,128)S(1)}, f32[2,512,4,512]{1,3,2,0:T(8,128)}) fusion(pred[512,512]{0,1:T(8,128)(4,1)S(1)} %and_or_fusion.2, bf16[512,2,4,80]{0,3,2,1:T(8,128)(2,1)} %bitcast.188, bf16[512,2,80]{0,2,1:T(8,128)(2,1)} %get-tuple-element.391), kind=kOutput, calls=%fused_computation.7.clone.1 | convolution fusion | flops 341831680 | bytes 9486336 | tf_op jit(solution)/shard_map/while/body/eval_jaxpr/nkgd,mkd->nkgm/dot_general | solution.py:34
  118.7 1.4 dynamic_update_slice.17
  120.1 4.6 %fusion.85 = f32[512,2,4]{0,2,1:T(4,128)S(1)} fusion(f32[2,512,4,512]{1,3,2,0:T(8,128)} %get-tuple-element.359, f32[512,2,4]{0,2,1:T(4,128)S(1)} %get-tuple-element.358, pred[512,512]{0,1:T(8,128)(4,1)S(1)} %and_or_fusion.2), kind=kLoop, calls=%fused_computation.12.clone.1 | loop fusion | flops 10481664 | bytes 8683520 | tf_op jit(solution)/shard_map/while/body/eval_jaxpr/reduce_sum | solution.py:41
  124.7 1.2 copy-done.1
  126.0 2.3 fusion.86
  128.3 2.4 copy.196
  130.8 24.2 %dynamic_update_slice.19 = f32[2,512,2,4,80]{1,0,4,3,2:T(2,128)} dynamic-update-slice(f32[2,512,2,4,80]{1,0,4,3,2:T(2,128)} %get-tuple-element.375, f32[1,512,2,4,80]{1,0,4,3,2:T(1,128)} %copy.196, s32[]{:T(128)S(6)} %copy.204, s32[]{:T(128)} %constant.138.clone.1..sunk, s32[]{:T(128)} %constant.138.clone.1..sunk, s32[]{:T(128)} %constant.138.clone.1..sunk, s32[]{:T(128)} %constant.138.clone.1..sunk) | dynamic-update-slice | bytes 2621444 | tf_op jit(solution)/shard_map/while/body/jit(dynamic_update_index_in_dim)/dynamic_update_slice | solution.py:126
  156.5 4.0 %all-to-all-start.1 = ((f32[8,128,2,4]{1,3,2,0:T(4,128)}), f32[8,128,2,4]{1,3,2,0:T(4,128)}, u32[]{:S(2)}, u32[]{:S(2)}) async-start(f32[8,128,2,4]{1,3,2,0:T(4,128)} %copy.135), calls=%async_computation.1 | async-start | bytes 65536 | tf_op jit(solution)/shard_map/all_to_all | solution.py:139
  161.1 1.0 copy.138
  162.1 1.8 gather_fusion
  165.4 4.1 %all-to-all-start.2 = ((f32[8,128,2,4]{1,3,2,0:T(4,128)}), f32[8,128,2,4]{1,3,2,0:T(4,128)S(1)}, u32[]{:S(2)}, u32[]{:S(2)}) async-start(f32[8,128,2,4]{1,3,2,0:T(4,128)} %copy.150), calls=%async_computation.2 | async-start | bytes 65536 | tf_op jit(solution)/shard_map/all_to_all | solution.py:140
  169.5 2.0 pad_maximum_fusion
  171.4 1.9 gather_fusion.1
  173.4 2.3 reshape.447
  175.7 3.7 reshape.446
  179.4 4.7 %reshape.442 = f32[8,128,2,4,80]{1,0,4,3,2:T(8,128)} reshape(f32[2,512,2,4,80]{1,0,4,3,2:T(2,128)} %get-tuple-element.70) | data formatting | bytes 5242880 | tf_op jit(solution)/shard_map/reshape | solution.py:136
  184.1 3.7 copy.133
  188.5 4.4 %all-to-all-start = ((f32[8,128,2,4,80]{1,4,3,2,0:T(8,128)}), f32[8,128,2,4,80]{1,4,3,2,0:T(8,128)}, u32[]{:S(2)}, u32[]{:S(2)}) async-start(f32[8,128,2,4,80]{1,4,3,2,0:T(8,128)} %copy.133), calls=%async_computation | async-start | bytes 5242880 | tf_op jit(solution)/shard_map/all_to_all | solution.py:141
  193.2 3.7 fusion.61
  196.9 1.4 fusion.65
  198.3 1.0 copy.160
  199.3 1.9 convolution_bitcast_fusion
  201.3 1.7 copy.146
  203.0 2.9 gather_fusion.3
  205.9 2.0 copy.148
  207.9 1.7 gather_fusion.2
  209.7 2.5 fusion.30
  212.2 1.1 copy.152
  213.3 1.4 gather_fusion.4
  214.7 1.0 copy.153
  217.3 7.9 %all-to-all-done = f32[8,128,2,4,80]{1,4,3,2,0:T(8,128)} async-done(((f32[8,128,2,4,80]{1,4,3,2,0:T(8,128)}), f32[8,128,2,4,80]{1,4,3,2,0:T(8,128)}, u32[]{:S(2)}, u32[]{:S(2)}) %all-to-all-start) | async-done | bytes 2621472 | tf_op jit(solution)/shard_map/all_to_all | solution.py:141
  225.2 2.1 multiply_reduce_fusion
  227.4 1.8 fusion.66
  229.5 59.2 %all-reduce.3.cloned.1.call-done = f32[128,2560]{1,0:T(8,128)} async-done(((f32[128,2560]{1,0:T(8,128)}), f32[128,2560]{1,0:T(8,128)}) %all-reduce.3.cloned.1.call-update) | async-done | bytes 1310736 | tf_op jit(solution)/shard_map/psum | solution.py:196
  288.7 1.8 fusion.24
  290.5 0.8 copy-done.3
  291.3 4.0 %fusion.45 = f32[128,896]{1,0:T(8,128)} fusion(bf16[2560,896]{1,0:T(8,128)(2,1)} %param.38, bf16[128,2560]{1,0:T(8,128)(2,1)S(1)} %get-tuple-element.228, f32[2560]{0:T(1024)S(1)} %convert_element_type.63, f32[128]{0:T(128)S(1)} %add_rsqrt_fusion.1), kind=kOutput, calls=%fused_computation.67 | convolution fusion | flops 588513280 | bytes 5712384 | tf_op jit(solution)/shard_map/dot_general | solution.py:199
  295.3 6.7 %fusion.29 = f32[128,2560]{1,0:T(8,128)} fusion(bf16[896,2560]{1,0:T(8,128)(2,1)} %param.40, bf16[2560,896]{1,0:T(8,128)(2,1)} %param.39, f32[128,896]{1,0:T(8,128)} %fusion.45, bf16[128,2560]{1,0:T(8,128)(2,1)} %copy-done.3, f32[2560]{0:T(1024)S(1)} %convert_element_type.63, f32[128]{0:T(128)S(1)} %add_rsqrt_fusion.1), kind=kOutput, calls=%fused_computation.50 | convolution fusion | flops 1176403968 | bytes 11610624 | tf_op jit(solution)/shard_map/dot_general | solution.py:202
  302.9 59.0 %all-reduce.5.cloned.1.call-done = f32[128,2560]{1,0:T(8,128)} async-done(((f32[128,2560]{1,0:T(8,128)}), f32[128,2560]{1,0:T(8,128)}) %all-reduce.5.cloned.1.call-update) | async-done | bytes 1310736 | tf_op jit(solution)/shard_map/psum | solution.py:202
  361.9 1.9 fusion.21
  363.8 2.7 convolution_convert_fusion.1
  366.6 1.4 convolution_convert_fusion
  (120 shorter events, 19.6 us)
Async XLA Ops:
  7.2 220.2 %copy-start = (bf16[640,2560]{1,0:T(8,128)(2,1)S(1)}, bf16[640,2560]{1,0:T(8,128)(2,1)}, u32[]{:S(2)}) copy-start(bf16[640,2560]{1,0:T(8,128)(2,1)} %param.36) | copy-start | bytes 9830404
  7.2 26.5 %copy-start.11 = (s32[4,128]{1,0:T(4,128)S(1)}, s32[4,128]{1,0:T(4,128)}, u32[]{:S(2)}) copy-start(s32[4,128]{1,0:T(4,128)} %constant.143.clone.1) | copy-start | bytes 6148
  7.2 12.8 %copy-start.14 = (s32[16]{0:T(128)S(1)}, s32[16]{0:T(128)}, u32[]{:S(2)}) copy-start(s32[16]{0:T(128)} %param.30) | copy-start | bytes 196
  7.2 13.4 %copy-start.19 = (s32[6]{0:T(128)S(1)}, s32[6]{0:T(128)}, u32[]{:S(2)}) copy-start(s32[6]{0:T(128)} %param.31) | copy-start | bytes 76
  7.2 13.5 %copy-start.15 = (s32[8]{0:T(128)S(1)}, s32[8]{0:T(128)}, u32[]{:S(2)}) copy-start(s32[8]{0:T(128)} %param.32) | copy-start | bytes 100
  7.2 25.0 %copy-start.5 = (s32[32]{0:T(128)S(1)}, s32[32]{0:T(128)}, u32[]{:S(2)}) copy-start(s32[32]{0:T(128)} %param.34) | copy-start | bytes 388
  7.2 30.9 %copy-start.20 = (s32[32]{0:T(128)S(1)}, s32[32]{0:T(128)}, u32[]{:S(2)}) copy-start(s32[32]{0:T(128)} %param.35) | copy-start | bytes 388
  7.2 47.4 %all-gather.2.cloned.1.call-start = ((), (), s32[]{:S(2)}) async-start(), calls=%async_computation.3 | async-start | bytes 1474560 | tf_op jit(solution)/shard_map/all_gather | solution.py:114
  15.7 5.0 %copy-start.21 = (s32[128]{0:T(128)}, s32[128]{0:T(128)S(1)}, u32[]{:S(2)}) copy-start(s32[128]{0:T(128)S(1)} %convert_reduce_fusion) | copy-start | bytes 1540
  69.9 5.8 %copy-start.1 = (f32[2,512,4,512]{1,3,2,0:T(8,128)S(1)}, f32[2,512,4,512]{1,3,2,0:T(8,128)}, u32[]{:S(2)}) copy-start(f32[2,512,4,512]{1,3,2,0:T(8,128)} %get-tuple-element.359) | copy-start | bytes 25165828 | tf_op jit(solution)/shard_map/while
  69.9 5.8 %copy-start.7 = (bf16[512,2,80]{0,2,1:T(8,128)(2,1)S(1)}, bf16[512,2,80]{0,2,1:T(8,128)(2,1)}, u32[]{:S(2)}) copy-start(bf16[512,2,80]{0,2,1:T(8,128)(2,1)} %get-tuple-element.392) | copy-start | bytes 491524 | tf_op jit(solution)/shard_map/while
  78.1 2.4 copy-start.9
  80.6 24.2 %copy-start.10 = (f32[2,512,2,4]{1,0,3,2:T(2,128)}, f32[2,512,2,4]{1,0,3,2:T(2,128)S(1)}, u32[]{:S(2)}) copy-start(f32[2,512,2,4]{1,0,3,2:T(2,128)S(1)} %dynamic_update_slice.18) | copy-start | bytes 98308 | tf_op jit(solution)/shard_map/while
  120.1 5.8 %copy-start.1 = (f32[2,512,4,512]{1,3,2,0:T(8,128)S(1)}, f32[2,512,4,512]{1,3,2,0:T(8,128)}, u32[]{:S(2)}) copy-start(f32[2,512,4,512]{1,3,2,0:T(8,128)} %get-tuple-element.359) | copy-start | bytes 25165828 | tf_op jit(solution)/shard_map/while
  120.1 5.8 %copy-start.7 = (bf16[512,2,80]{0,2,1:T(8,128)(2,1)S(1)}, bf16[512,2,80]{0,2,1:T(8,128)(2,1)}, u32[]{:S(2)}) copy-start(bf16[512,2,80]{0,2,1:T(8,128)(2,1)} %get-tuple-element.392) | copy-start | bytes 491524 | tf_op jit(solution)/shard_map/while
  128.3 2.4 copy-start.9
  130.8 24.2 %copy-start.10 = (f32[2,512,2,4]{1,0,3,2:T(2,128)}, f32[2,512,2,4]{1,0,3,2:T(2,128)S(1)}, u32[]{:S(2)}) copy-start(f32[2,512,2,4]{1,0,3,2:T(2,128)S(1)} %dynamic_update_slice.18) | copy-start | bytes 98308 | tf_op jit(solution)/shard_map/while
  155.1 16.4 %copy-start.2 = (bf16[128,640]{1,0:T(8,128)(2,1)S(1)}, bf16[128,640]{1,0:T(8,128)(2,1)}, u32[]{:S(2)}) copy-start(bf16[128,640]{1,0:T(8,128)(2,1)} %param.24) | copy-start | bytes 491524
  156.5 8.8 %all-to-all-start.1 = ((f32[8,128,2,4]{1,3,2,0:T(4,128)}), f32[8,128,2,4]{1,3,2,0:T(4,128)}, u32[]{:S(2)}, u32[]{:S(2)}) async-start(f32[8,128,2,4]{1,3,2,0:T(4,128)} %copy.135), calls=%async_computation.1 | async-start | bytes 65536 | tf_op jit(solution)/shard_map/all_to_all | solution.py:139
  165.4 22.5 %all-to-all-start.2 = ((f32[8,128,2,4]{1,3,2,0:T(4,128)}), f32[8,128,2,4]{1,3,2,0:T(4,128)S(1)}, u32[]{:S(2)}, u32[]{:S(2)}) async-start(f32[8,128,2,4]{1,3,2,0:T(4,128)} %copy.150), calls=%async_computation.2 | async-start | bytes 65536 | tf_op jit(solution)/shard_map/all_to_all | solution.py:140
  187.9 5.1 %copy-start.16 = (s32[16]{0:T(128)S(1)}, s32[16]{0:T(128)}, u32[]{:S(2)}) copy-start(s32[16]{0:T(128)} %param.28) | copy-start | bytes 196
  187.9 0.6 copy-start.8
  188.5 36.7 %all-to-all-start = ((f32[8,128,2,4,80]{1,4,3,2,0:T(8,128)}), f32[8,128,2,4,80]{1,4,3,2,0:T(8,128)}, u32[]{:S(2)}, u32[]{:S(2)}) async-start(f32[8,128,2,4,80]{1,4,3,2,0:T(8,128)} %copy.133), calls=%async_computation | async-start | bytes 5242880 | tf_op jit(solution)/shard_map/all_to_all | solution.py:141
  192.9 95.8 %all-reduce.3.cloned.1.call-start = ((), (), s32[]{:S(2)}) async-start(), calls=%async_computation.4 | async-start | bytes 2621440 | tf_op jit(solution)/shard_map/psum | solution.py:196
  193.0 4.0 %copy-start.6 = (bf16[16,16,2,4,80]{4,3,2,1,0:T(4,128)(2,1)S(1)}, bf16[16,16,2,4,80]{4,3,2,1,0:T(4,128)(2,1)}, u32[]{:S(2)}) copy-start(bf16[16,16,2,4,80]{4,3,2,1,0:T(4,128)(2,1)} %reshape.447) | copy-start | bytes 983044
  201.2 1.8 copy-start.17
  201.2 1.8 copy-start.22
  225.2 2.1 copy-start.4
  227.3 2.1 copy-start.12
  229.2 132.7 %all-reduce.5.cloned.1.call-start = ((), (), s32[]{:S(2)}) async-start(), calls=%async_computation.5 | async-start | bytes 2621440 | tf_op jit(solution)/shard_map/psum | solution.py:202
  290.5 0.9 copy-start.3
  295.3 6.8 %copy-start.13 = (bf16[2560]{0:T(1024)(128)(2,1)S(1)}, bf16[2560]{0:T(1024)(128)(2,1)}, u32[]{:S(2)}) copy-start(bf16[2560]{0:T(1024)(128)(2,1)} %param.41) | copy-start | bytes 15364
  361.9 4.7 %copy-start.18 = (bf16[2560,640]{1,0:T(8,128)(2,1)S(1)}, bf16[2560,640]{1,0:T(8,128)(2,1)}, u32[]{:S(2)}) copy-start(bf16[2560,640]{1,0:T(8,128)(2,1)} %param.42) | copy-start | bytes 9830404
Sparse Core Ops, SparseCore 0:
  10.0 27.2 all-gather.1
  229.3 59.3 all-reduce.2
  302.2 59.6 all-reduce.4
where the time goes:
time: 381 us; the launch traced here: 375 us
  waiting for transfers between devices  127 us (33%)
  local copies, waits for them, and re-layouts  125 us (33%)
  other arithmetic  49 us (13%)
  matrix products  36.3 us (10%)
  between operations  14.1 us (4%)
  starting transfers between devices  12.8 us (3%)
  blocking collectives  11.4 us (3%)
    psum x1, waiting for transfers between devices, per_device(): lax.psum(jnp.dot(attention, out_weight, preferred_element_type=jnp.float3...  59.2 us
    psum x1, waiting for transfers between devices, per_device(): lax.psum(jnp.dot(hidden, down_weight, preferred_element_type=jnp.float32)...  59 us
    dynamic_update_slice x12, local copies, waits for them, and re-layouts, visit_owners(): lax.map(owner_block, (all_query.reshape(total_rows // block, block, all_q...  57.6 us
    select_n x1, other arithmetic, pool_split(): jnp.repeat(node_of_page, page_size, total_repeat_length=page_count * page...  16 us
    dot_general x3, matrix products, attend(): jnp.einsum('nkgd,mkd->nkgm', queries, keys, preferred_element_type=jnp.fl...  13.1 us
    reduce_sum x3, other arithmetic, attend(): total = jnp.sum(raised, axis=-1)  11.8 us
    all_gather x1, blocking collectives, visit_owners(): lax.all_gather(token_info, 'req', axis=0, tiled=True)  11.4 us
    reshape x6, local copies, waits for them, and re-layouts, visit_owners(): item.reshape((holders, row_count) + item.shape[2:])  11.4 us
  transfers between devices with their start and end apart: 6, of which 3 were waited for; matrix products, arithmetic and copies ran while one was open for 22% of the time, Pallas kernels for 0%

commit v1 on v0

--- a/solution.py
+++ b/solution.py
@@ -110,9 +110,20 @@
 
 
 def visit_owners(new_query, token_info, prefix_pool, page_node, page_rank, kv_local, group):
+
+    def _push_packet(page):
+        row_list = []
+        for _ in range(lax.axis_size("req")):
+            row_list.append(page)
+        a_now = jnp.concatenate(
+            lax.all_to_all(jnp.stack(row_list), axis_name="req", split_axis=0, concat_axis=0),
+            axis=0,
+        )
+        return a_now
+
     all_query, all_info = (
         lax.all_gather(new_query, "req", axis=0, tiled=True),
-        lax.all_gather(token_info, "req", axis=0, tiled=True),
+        _push_packet(token_info),
     )
     total_rows = all_query.shape[0]
     block = math.gcd(total_rows, 512)

time: 381 us -> 382 us (level)
  blocking collectives: 11.4 us -> 0 us
  starting transfers between devices: 12.8 us -> 18.3 us
    all_gather x1 -> x0, blocking collectives: 11.4 us -> none  [visit_owners(): lax.all_gather(token_info, 'req', axis=0, tiled=True)]
    all_to_all x0 -> x1, starting transfers between devices: none -> 5.17 us  [_push_packet(): lax.all_to_all(jnp.stack(row_list), axis_name='req', split_axis=0, concat...]
  transfers between devices with their start and end apart: 6 -> 7, of which waited for: 3 -> 4; matrix products, arithmetic and copies ran while one was open for 22% -> 24% of each run, Pallas kernels for 0% -> 0%
where the time goes in v1:
time: 382 us; the launch traced here: 377 us
  local copies, waits for them, and re-layouts  128 us (34%)
  waiting for transfers between devices  127 us (33%)
  other arithmetic  52.7 us (14%)
  matrix products  36.3 us (10%)
  starting transfers between devices  18.3 us (5%)
  between operations  14 us (4%)
    psum x1, waiting for transfers between devices, per_device(): lax.psum(jnp.dot(attention, out_weight, preferred_element_type=jnp.float3...  59.4 us
    psum x1, waiting for transfers between devices, per_device(): lax.psum(jnp.dot(hidden, down_weight, preferred_element_type=jnp.float32)...  59 us
    dynamic_update_slice x12, local copies, waits for them, and re-layouts, visit_owners(): lax.map(owner_block, (all_query.reshape(total_rows // block, block, all_q...  57.6 us
    select_n x1, other arithmetic, pool_split(): jnp.repeat(node_of_page, page_size, total_repeat_length=page_count * page...  16.7 us
    dot_general x3, matrix products, attend(): jnp.einsum('nkgd,mkd->nkgm', queries, keys, preferred_element_type=jnp.fl...  13.1 us
    reduce_sum x3, other arithmetic, attend(): total = jnp.sum(raised, axis=-1)  11.8 us
    reshape x6, local copies, waits for them, and re-layouts, visit_owners(): item.reshape((holders, row_count) + item.shape[2:])  11.4 us
    gather x6, local copies, waits for them, and re-layouts, local_part(): item.reshape((requests * MAXNEW,) + item.shape[2:])[flat]  8.97 us
  transfers between devices with their start and end apart: 7, of which 4 were waited for; matrix products, arithmetic and copies ran while one was open for 24% of the time, Pallas kernels for 0%

profile of v1, /device:TPU:0, one launch (start us, length us, event | category | flops | bytes accessed | tf_op | source)
XLA Modules:
  0.0 376.6 jit_solution(4011879178154455613)
XLA Ops:
  10.2 1.2 select_reduce_fusion.1
  13.6 5.2 %all-to-all-start = ((s32[8,128,4]{1,2,0:T(4,128)}), s32[8,128,4]{1,2,0:T(4,128)}, u32[]{:S(2)}, u32[]{:S(2)}) async-start(s32[8,128,4]{1,2,0:T(4,128)} %stack.28), calls=%async_computation | async-start | bytes 32768 | tf_op jit(solution)/shard_map/all_to_all | solution.py:119
  18.8 2.1 reshape.439
  20.9 1.8 fusion.64
  22.7 2.1 fusion.63
  25.5 4.3 %compare_select_fusion.2 = (s32[512,1]{0,1:T(1,128)S(1)}, s32[512,1]{0,1:T(1,128)S(1)}) fusion(s32[]{:T(128)} %bitcast.29, s32[]{:T(128)} %bitcast.30, s32[]{:T(128)} %bitcast.31, s32[]{:T(128)} %bitcast.32, s32[]{:T(128)} %bitcast.33, s32[]{:T(128)} %bitcast.35, s32[]{:T(128)} %bitcast.34, s32[512,1]{0,1:T(1,128)S(1)} %bitcast.213, s32[512,1]{0,1:T(1,128)S(1)} %bitcast.212), kind=kLoop, calls=%fused_computation.105 | loop fusion | flops 7168 | bytes 8220 | tf_op jit(solution)/shard_map/jit(_take)/gather | solution.py:52
  30.7 16.7 %select_select_fusion = s32[512]{0:T(512)} fusion(pred[512]{0:T(512)(128)(4,1)S(1)} %get-tuple-element.190, pred[512]{0:T(512)(128)(4,1)S(1)} %get-tuple-element.189, pred[512]{0:T(512)(128)(4,1)S(1)} %get-tuple-element.188, pred[512]{0:T(512)(128)(4,1)S(1)} %get-tuple-element.187, pred[512]{0:T(512)(128)(4,1)S(1)} %get-tuple-element.186, ...), kind=kLoop, calls=%fused_computation.129 | loop fusion | flops 17408 | bytes 19060 | tf_op jit(solution)/shard_map/jit(_take)/select_n | solution.py:52
  47.4 3.1 fusion.62
  51.7 1.8 copy.132
  53.6 1.8 copy.131
  55.4 100.6 %while.16 = (s32[]{:T(128)}, f32[2,512,2,4]{1,0,3,2:T(2,128)}, f32[2,512,2,4]{1,0,3,2:T(2,128)}, f32[2,512,2,4,80]{1,0,4,3,2:T(2,128)}, s32[512]{0:T(512)}, /*in...) while((s32[]{:T(128)}, f32[2,512,2,4]{1,0,3,2:T(2,128)}, ...), condition=%wide.region_9.10_spmd.clone, body=%wide.region_6.0_spmd.clone.sunk | while | flops 700178944 | bytes 71092600 | solution.py:137
  57.5 1.2 and_or_fusion.2
  58.7 2.0 constant_dynamic-slice_fusion.3
  60.7 2.2 copy.196
  62.9 5.8 %bitcast_reduce_fusion.2 = (f32[512,2,4]{0,2,1:T(4,128)S(1)}, f32[2,512,4,512]{1,3,2,0:T(8,128)}) fusion(pred[512,512]{0,1:T(8,128)(4,1)S(1)} %and_or_fusion.2, bf16[512,2,4,80]{0,3,2,1:T(8,128)(2,1)} %bitcast.188, bf16[512,2,80]{0,2,1:T(8,128)(2,1)} %get-tuple-element.381), kind=kOutput, calls=%fused_computation.7.clone.1 | convolution fusion | flops 341831680 | bytes 9486336 | tf_op jit(solution)/shard_map/while/body/eval_jaxpr/nkgd,mkd->nkgm/dot_general | solution.py:34
  69.3 1.4 dynamic_update_slice.17
  70.8 4.6 %fusion.85 = f32[512,2,4]{0,2,1:T(4,128)S(1)} fusion(f32[2,512,4,512]{1,3,2,0:T(8,128)} %get-tuple-element.349, f32[512,2,4]{0,2,1:T(4,128)S(1)} %get-tuple-element.348, pred[512,512]{0,1:T(8,128)(4,1)S(1)} %and_or_fusion.2), kind=kLoop, calls=%fused_computation.12.clone.1 | loop fusion | flops 10481664 | bytes 8683520 | tf_op jit(solution)/shard_map/while/body/eval_jaxpr/reduce_sum | solution.py:41
  75.4 1.2 copy-done.1
  76.6 2.3 fusion.86
  78.9 2.4 copy.199
  81.5 24.2 %dynamic_update_slice.19 = f32[2,512,2,4,80]{1,0,4,3,2:T(2,128)} dynamic-update-slice(f32[2,512,2,4,80]{1,0,4,3,2:T(2,128)} %get-tuple-element.365, f32[1,512,2,4,80]{1,0,4,3,2:T(1,128)} %copy.199, s32[]{:T(128)S(6)} %copy.207, s32[]{:T(128)} %constant.138.clone.1..sunk, s32[]{:T(128)} %constant.138.clone.1..sunk, s32[]{:T(128)} %constant.138.clone.1..sunk, s32[]{:T(128)} %constant.138.clone.1..sunk) | dynamic-update-slice | bytes 2621444 | tf_op jit(solution)/shard_map/while/body/jit(dynamic_update_index_in_dim)/dynamic_update_slice | solution.py:137
  107.8 1.2 and_or_fusion.2
  109.0 2.0 constant_dynamic-slice_fusion.3
  111.0 2.2 copy.196
  113.2 5.8 %bitcast_reduce_fusion.2 = (f32[512,2,4]{0,2,1:T(4,128)S(1)}, f32[2,512,4,512]{1,3,2,0:T(8,128)}) fusion(pred[512,512]{0,1:T(8,128)(4,1)S(1)} %and_or_fusion.2, bf16[512,2,4,80]{0,3,2,1:T(8,128)(2,1)} %bitcast.188, bf16[512,2,80]{0,2,1:T(8,128)(2,1)} %get-tuple-element.381), kind=kOutput, calls=%fused_computation.7.clone.1 | convolution fusion | flops 341831680 | bytes 9486336 | tf_op jit(solution)/shard_map/while/body/eval_jaxpr/nkgd,mkd->nkgm/dot_general | solution.py:34
  119.6 1.4 dynamic_update_slice.17
  121.0 4.6 %fusion.85 = f32[512,2,4]{0,2,1:T(4,128)S(1)} fusion(f32[2,512,4,512]{1,3,2,0:T(8,128)} %get-tuple-element.349, f32[512,2,4]{0,2,1:T(4,128)S(1)} %get-tuple-element.348, pred[512,512]{0,1:T(8,128)(4,1)S(1)} %and_or_fusion.2), kind=kLoop, calls=%fused_computation.12.clone.1 | loop fusion | flops 10481664 | bytes 8683520 | tf_op jit(solution)/shard_map/while/body/eval_jaxpr/reduce_sum | solution.py:41
  125.7 1.2 copy-done.1
  126.9 2.3 fusion.86
  129.2 2.4 copy.199
  131.8 24.2 %dynamic_update_slice.19 = f32[2,512,2,4,80]{1,0,4,3,2:T(2,128)} dynamic-update-slice(f32[2,512,2,4,80]{1,0,4,3,2:T(2,128)} %get-tuple-element.365, f32[1,512,2,4,80]{1,0,4,3,2:T(1,128)} %copy.199, s32[]{:T(128)S(6)} %copy.207, s32[]{:T(128)} %constant.138.clone.1..sunk, s32[]{:T(128)} %constant.138.clone.1..sunk, s32[]{:T(128)} %constant.138.clone.1..sunk, s32[]{:T(128)} %constant.138.clone.1..sunk) | dynamic-update-slice | bytes 2621444 | tf_op jit(solution)/shard_map/while/body/jit(dynamic_update_index_in_dim)/dynamic_update_slice | solution.py:137
  157.4 4.2 %all-to-all-start.2 = ((f32[8,128,2,4]{1,3,2,0:T(4,128)}), f32[8,128,2,4]{1,3,2,0:T(4,128)}, u32[]{:S(2)}, u32[]{:S(2)}) async-start(f32[8,128,2,4]{1,3,2,0:T(4,128)} %copy.138), calls=%async_computation.2 | async-start | bytes 65536 | tf_op jit(solution)/shard_map/all_to_all | solution.py:150
  162.3 1.0 copy.141
  163.3 1.8 gather_fusion
  166.6 4.1 %all-to-all-start.3 = ((f32[8,128,2,4]{1,3,2,0:T(4,128)}), f32[8,128,2,4]{1,3,2,0:T(4,128)S(1)}, u32[]{:S(2)}, u32[]{:S(2)}) async-start(f32[8,128,2,4]{1,3,2,0:T(4,128)} %copy.153), calls=%async_computation.3 | async-start | bytes 65536 | tf_op jit(solution)/shard_map/all_to_all | solution.py:151
  170.7 2.0 pad_maximum_fusion
  172.7 1.9 gather_fusion.1
  174.6 2.3 reshape.445
  177.0 3.7 reshape.444
  180.7 4.7 %reshape.440 = f32[8,128,2,4,80]{1,0,4,3,2:T(8,128)} reshape(f32[2,512,2,4,80]{1,0,4,3,2:T(2,128)} %get-tuple-element.70) | data formatting | bytes 5242880 | tf_op jit(solution)/shard_map/reshape | solution.py:147
  185.4 3.7 copy.136
  189.8 4.4 %all-to-all-start.1 = ((f32[8,128,2,4,80]{1,4,3,2,0:T(8,128)}), f32[8,128,2,4,80]{1,4,3,2,0:T(8,128)}, u32[]{:S(2)}, u32[]{:S(2)}) async-start(f32[8,128,2,4,80]{1,4,3,2,0:T(8,128)} %copy.136), calls=%async_computation.1 | async-start | bytes 5242880 | tf_op jit(solution)/shard_map/all_to_all | solution.py:152
  194.5 3.7 fusion.61
  198.2 1.4 fusion.65
  200.6 1.9 convolution_bitcast_fusion
  202.6 1.7 copy.149
  204.3 2.9 gather_fusion.3
  207.2 2.0 copy.151
  209.1 1.7 gather_fusion.2
  210.9 2.5 fusion.30
  213.5 1.1 copy.155
  214.6 1.4 gather_fusion.4
  216.0 1.0 copy.156
  218.6 7.9 %all-to-all-done.1 = f32[8,128,2,4,80]{1,4,3,2,0:T(8,128)} async-done(((f32[8,128,2,4,80]{1,4,3,2,0:T(8,128)}), f32[8,128,2,4,80]{1,4,3,2,0:T(8,128)}, u32[]{:S(2)}, u32[]{:S(2)}) %all-to-all-start.1) | async-done | bytes 2621472 | tf_op jit(solution)/shard_map/all_to_all | solution.py:152
  226.5 2.1 multiply_reduce_fusion
  228.6 1.8 fusion.66
  230.7 59.4 %all-reduce.3.cloned.1.call-done = f32[128,2560]{1,0:T(8,128)} async-done(((f32[128,2560]{1,0:T(8,128)}), f32[128,2560]{1,0:T(8,128)}) %all-reduce.3.cloned.1.call-update) | async-done | bytes 1310736 | tf_op jit(solution)/shard_map/psum | solution.py:207
  290.1 1.8 fusion.24
  292.7 4.0 %fusion.45 = f32[128,896]{1,0:T(8,128)} fusion(bf16[2560,896]{1,0:T(8,128)(2,1)} %param.38, bf16[128,2560]{1,0:T(8,128)(2,1)S(1)} %get-tuple-element.218, f32[2560]{0:T(1024)S(1)} %convert_element_type.63, f32[128]{0:T(128)S(1)} %add_rsqrt_fusion.1), kind=kOutput, calls=%fused_computation.67 | convolution fusion | flops 588513280 | bytes 5712384 | tf_op jit(solution)/shard_map/dot_general | solution.py:210
  296.7 6.7 %fusion.29 = f32[128,2560]{1,0:T(8,128)} fusion(bf16[896,2560]{1,0:T(8,128)(2,1)} %param.40, bf16[2560,896]{1,0:T(8,128)(2,1)} %param.39, f32[128,896]{1,0:T(8,128)} %fusion.45, bf16[128,2560]{1,0:T(8,128)(2,1)} %copy-done.3, f32[2560]{0:T(1024)S(1)} %convert_element_type.63, f32[128]{0:T(128)S(1)} %add_rsqrt_fusion.1), kind=kOutput, calls=%fused_computation.50 | convolution fusion | flops 1176403968 | bytes 11610624 | tf_op jit(solution)/shard_map/dot_general | solution.py:213
  304.3 59.0 %all-reduce.5.cloned.1.call-done = f32[128,2560]{1,0:T(8,128)} async-done(((f32[128,2560]{1,0:T(8,128)}), f32[128,2560]{1,0:T(8,128)}) %all-reduce.5.cloned.1.call-update) | async-done | bytes 1310736 | tf_op jit(solution)/shard_map/psum | solution.py:213
  363.3 1.9 fusion.21
  365.3 2.7 convolution_convert_fusion.1
  368.0 1.4 convolution_convert_fusion
  (112 shorter events, 23.6 us)
Async XLA Ops:
  7.2 221.4 %copy-start = (bf16[640,2560]{1,0:T(8,128)(2,1)S(1)}, bf16[640,2560]{1,0:T(8,128)(2,1)}, u32[]{:S(2)}) copy-start(bf16[640,2560]{1,0:T(8,128)(2,1)} %param.36) | copy-start | bytes 9830404
  7.2 43.3 %copy-start.15 = (s32[32]{0:T(128)S(1)}, s32[32]{0:T(128)}, u32[]{:S(2)}) copy-start(s32[32]{0:T(128)} %param.35) | copy-start | bytes 388
  7.2 48.2 %all-gather.2.cloned.1.call-start = ((), (), s32[]{:S(2)}) async-start(), calls=%async_computation.4 | async-start | bytes 1474560 | tf_op jit(solution)/shard_map/all_gather | solution.py:125
  9.7 0.5 copy-start.16
  13.6 41.8 %all-to-all-start = ((s32[8,128,4]{1,2,0:T(4,128)}), s32[8,128,4]{1,2,0:T(4,128)}, u32[]{:S(2)}, u32[]{:S(2)}) async-start(s32[8,128,4]{1,2,0:T(4,128)} %stack.28), calls=%async_computation | async-start | bytes 32768 | tf_op jit(solution)/shard_map/all_to_all | solution.py:119
  70.8 5.8 %copy-start.1 = (f32[2,512,4,512]{1,3,2,0:T(8,128)S(1)}, f32[2,512,4,512]{1,3,2,0:T(8,128)}, u32[]{:S(2)}) copy-start(f32[2,512,4,512]{1,3,2,0:T(8,128)} %get-tuple-element.349) | copy-start | bytes 25165828 | tf_op jit(solution)/shard_map/while
  70.8 5.8 %copy-start.6 = (bf16[512,2,80]{0,2,1:T(8,128)(2,1)S(1)}, bf16[512,2,80]{0,2,1:T(8,128)(2,1)}, u32[]{:S(2)}) copy-start(bf16[512,2,80]{0,2,1:T(8,128)(2,1)} %get-tuple-element.382) | copy-start | bytes 491524 | tf_op jit(solution)/shard_map/while
  78.9 2.4 copy-start.8
  81.5 24.2 %copy-start.9 = (f32[2,512,2,4]{1,0,3,2:T(2,128)}, f32[2,512,2,4]{1,0,3,2:T(2,128)S(1)}, u32[]{:S(2)}) copy-start(f32[2,512,2,4]{1,0,3,2:T(2,128)S(1)} %dynamic_update_slice.18) | copy-start | bytes 98308 | tf_op jit(solution)/shard_map/while
  121.0 5.8 %copy-start.1 = (f32[2,512,4,512]{1,3,2,0:T(8,128)S(1)}, f32[2,512,4,512]{1,3,2,0:T(8,128)}, u32[]{:S(2)}) copy-start(f32[2,512,4,512]{1,3,2,0:T(8,128)} %get-tuple-element.349) | copy-start | bytes 25165828 | tf_op jit(solution)/shard_map/while
  121.0 5.8 %copy-start.6 = (bf16[512,2,80]{0,2,1:T(8,128)(2,1)S(1)}, bf16[512,2,80]{0,2,1:T(8,128)(2,1)}, u32[]{:S(2)}) copy-start(bf16[512,2,80]{0,2,1:T(8,128)(2,1)} %get-tuple-element.382) | copy-start | bytes 491524 | tf_op jit(solution)/shard_map/while
  129.2 2.4 copy-start.8
  131.8 24.2 %copy-start.9 = (f32[2,512,2,4]{1,0,3,2:T(2,128)}, f32[2,512,2,4]{1,0,3,2:T(2,128)S(1)}, u32[]{:S(2)}) copy-start(f32[2,512,2,4]{1,0,3,2:T(2,128)S(1)} %dynamic_update_slice.18) | copy-start | bytes 98308 | tf_op jit(solution)/shard_map/while
  156.0 16.7 %copy-start.2 = (bf16[128,640]{1,0:T(8,128)(2,1)S(1)}, bf16[128,640]{1,0:T(8,128)(2,1)}, u32[]{:S(2)}) copy-start(bf16[128,640]{1,0:T(8,128)(2,1)} %param.24) | copy-start | bytes 491524
  157.4 9.2 %all-to-all-start.2 = ((f32[8,128,2,4]{1,3,2,0:T(4,128)}), f32[8,128,2,4]{1,3,2,0:T(4,128)}, u32[]{:S(2)}, u32[]{:S(2)}) async-start(f32[8,128,2,4]{1,3,2,0:T(4,128)} %copy.138), calls=%async_computation.2 | async-start | bytes 65536 | tf_op jit(solution)/shard_map/all_to_all | solution.py:150
  166.6 22.6 %all-to-all-start.3 = ((f32[8,128,2,4]{1,3,2,0:T(4,128)}), f32[8,128,2,4]{1,3,2,0:T(4,128)S(1)}, u32[]{:S(2)}, u32[]{:S(2)}) async-start(f32[8,128,2,4]{1,3,2,0:T(4,128)} %copy.153), calls=%async_computation.3 | async-start | bytes 65536 | tf_op jit(solution)/shard_map/all_to_all | solution.py:151
  189.2 5.1 %copy-start.12 = (s32[16]{0:T(128)S(1)}, s32[16]{0:T(128)}, u32[]{:S(2)}) copy-start(s32[16]{0:T(128)} %param.28) | copy-start | bytes 196
  189.2 0.6 copy-start.7
  189.8 36.7 %all-to-all-start.1 = ((f32[8,128,2,4,80]{1,4,3,2,0:T(8,128)}), f32[8,128,2,4,80]{1,4,3,2,0:T(8,128)}, u32[]{:S(2)}, u32[]{:S(2)}) async-start(f32[8,128,2,4,80]{1,4,3,2,0:T(8,128)} %copy.136), calls=%async_computation.1 | async-start | bytes 5242880 | tf_op jit(solution)/shard_map/all_to_all | solution.py:152
  194.2 96.0 %all-reduce.3.cloned.1.call-start = ((), (), s32[]{:S(2)}) async-start(), calls=%async_computation.5 | async-start | bytes 2621440 | tf_op jit(solution)/shard_map/psum | solution.py:207
  194.2 4.0 %copy-start.5 = (bf16[16,16,2,4,80]{4,3,2,1,0:T(4,128)(2,1)S(1)}, bf16[16,16,2,4,80]{4,3,2,1,0:T(4,128)(2,1)}, u32[]{:S(2)}) copy-start(bf16[16,16,2,4,80]{4,3,2,1,0:T(4,128)(2,1)} %reshape.445) | copy-start | bytes 983044
  202.5 1.8 copy-start.13
  202.5 1.8 copy-start.17
  226.5 2.1 copy-start.4
  228.6 2.1 copy-start.10
  230.4 132.9 %all-reduce.5.cloned.1.call-start = ((), (), s32[]{:S(2)}) async-start(), calls=%async_computation.6 | async-start | bytes 2621440 | tf_op jit(solution)/shard_map/psum | solution.py:213
  291.9 0.9 copy-start.3
  296.7 6.8 %copy-start.11 = (bf16[2560]{0:T(1024)(128)(2,1)S(1)}, bf16[2560]{0:T(1024)(128)(2,1)}, u32[]{:S(2)}) copy-start(bf16[2560]{0:T(1024)(128)(2,1)} %param.41) | copy-start | bytes 15364
  363.3 4.7 %copy-start.14 = (bf16[2560,640]{1,0:T(8,128)(2,1)S(1)}, bf16[2560,640]{1,0:T(8,128)(2,1)}, u32[]{:S(2)}) copy-start(bf16[2560,640]{1,0:T(8,128)(2,1)} %param.42) | copy-start | bytes 9830404
Sparse Core Ops, SparseCore 0:
  9.9 27.3 all-gather.1
  230.6 59.5 all-reduce.2
  303.6 59.6 all-reduce.4
